TPU v7x, 512 devices: a whole 4x4x16 slice. The times are simulated.
512 devices in a mesh: seq: 64 (over y_lo, z, core), kv: 8 (over x, y_hi).
Axes of the slice: x: 4, y: 4 (y_hi: 2, y_lo: 2; y = y_hi * 2 + y_lo), z: 16, core: 2. Of those that a mesh axis runs over, the one named last changes fastest.
Arguments:
- queries: bfloat16 [64, 16384, 128], P('kv', 'seq'), may hold values from -56 to 56
- key_states: bfloat16 [8, 16384, 128], P('kv', 'seq'), may hold values from -56 to 56
- samples: int32 [64, 512], P('kv', 'seq'), may hold values from 0 to 16383, as said below
- query_gate_weight: float32 [128, 128], replicated, may hold values from -6 to 6
- key_gate_weight: float32 [384, 128], replicated, may hold values from -0.3125 to 0.3125
Outputs:
- row_loss: float32 [64, 512], P('kv', 'seq')
- query_grad: float32 [128, 128], replicated
- key_grad: float32 [384, 128], replicated
Inputs may be any that keep to these rules, and one draw needn't show every extreme that they name: `samples`: sampled row r of every head lies in the tokens r // 8 * 256 to (r // 8 + 1) * 256 - 1; positions may repeat.
All inputs are finite; a program needn't handle non-finite values.
Results may differ from a plain program's by a relative error of at most 0.0003.
Values may be sent and summed in bfloat16 or wider, within the bound.
A program may use at most 64 MiB of HBM per device.

v0:
```python
import math
import jax
import jax.numpy as jnp
from jax import lax
from jax.sharding import Mesh
from jax.sharding import PartitionSpec as P

BLOCK = 128
SEQ = ("seq_0", "seq_1", "seq_2")
SEQ_KV = ("seq_0", "seq_1", "seq_2", "kv")
masked_score = -1e30
highest = lax.Precision.HIGHEST


def laid_out(tiles, dim):
    shape = list(tiles.shape[1:])
    shape[dim] *= tiles.shape[0]
    return jnp.moveaxis(tiles, 0, dim).reshape(shape)


def gather_in_order(array, axes, sequence):
    tiles = array[None]
    for k in sequence:
        tiles = lax.all_gather(tiles, axes[k], axis=0, tiled=True)
    held = [lax.axis_size(axes[k]) for k in reversed(sequence)]
    tiles = tiles.reshape(*held, *array.shape)
    turned = sorted(range(len(sequence)), key=lambda place: sequence[len(sequence) - 1 - place])
    return tiles.transpose(*turned, *range(len(sequence), tiles.ndim)).reshape(-1, *array.shape)


def gathered_by_axis(array, axes, sequence, dim):
    return laid_out(gather_in_order(array, axes, sequence), dim)


def from_everyone(array, axis):
    copies = jnp.broadcast_to(array, (lax.axis_size(axis), *array.shape))
    return lax.all_to_all(copies, axis, split_axis=0, concat_axis=0, tiled=True)


def gather_directly(array, axis, dim):
    return laid_out(from_everyone(array, axis), dim)


def in_blocks(array, dim, peers):
    shape = array.shape
    tiles = array.reshape(*shape[:dim], peers, shape[dim] // peers, *shape[dim + 1 :])
    return jnp.moveaxis(tiles, dim, 0)


def sent_and_summed(array, axis, dim):
    tiles = in_blocks(array, dim, lax.axis_size(axis))
    arrived = lax.all_to_all(tiles, axis, split_axis=0, concat_axis=0, tiled=True)
    return arrived.sum(axis=0)


def in_one(arrays, axis):
    ends = [0]
    for a in arrays:
        ends.append(ends[-1] + a.size)
    so_far = lax.psum(jnp.concatenate([a.ravel() for a in arrays]), axis)
    return tuple((so_far[b:e].reshape(a.shape) for a, b, e in zip(arrays, ends, ends[1:])))


def score_tile(row_block, key_block):
    return lax.dot_general(
        row_block, key_block, (((1,), (1,)), ((), ())), preferred_element_type=jnp.float32
    )


def body(queries, key_states, samples, query_gate_weight, key_gate_weight):
    head_count, shard_len, head_width = queries.shape
    rows_local = samples.shape[1]
    gate_width = query_gate_weight.shape[1]
    seq_devices = lax.axis_size(SEQ)
    shard_index = lax.axis_index(SEQ)
    offset = shard_index * shard_len
    local_blocks = shard_len // BLOCK
    total_blocks = local_blocks * seq_devices
    score_scale = 1.0 / math.sqrt(head_width)
    gate_scale = 1.0 / math.sqrt(gate_width)
    pooled_query = jnp.mean(
        queries.reshape(head_count, local_blocks, BLOCK, head_width), axis=2, dtype=jnp.float32
    )
    key_rows = key_states[0]
    key_blocks = key_rows.reshape(local_blocks, BLOCK, head_width)
    pooled_key = jnp.concatenate(
        [
            jnp.max(key_blocks, axis=1).astype(jnp.float32),
            jnp.min(key_blocks, axis=1).astype(jnp.float32),
            jnp.mean(key_blocks, axis=1, dtype=jnp.float32),
        ],
        axis=-1,
    )
    gate_key = jnp.dot(pooled_key, key_gate_weight, precision=highest)
    local_places = samples - offset
    query_rows = jnp.take_along_axis(queries, local_places[:, :, None], axis=1)
    row_count = head_count * rows_local
    flat_rows = query_rows.reshape(row_count, head_width)
    flat_places = samples.reshape(row_count)
    initial = (
        jnp.full((row_count,), masked_score, jnp.float32),
        jnp.zeros((row_count, total_blocks), jnp.float32),
    )
    pieces = gathered_by_axis(key_rows, SEQ, (0, 1, 2), 0).reshape(-1, shard_len, head_width)

    def absorb_one(turn_number, running):
        running_top, running_mass = running
        first_key = turn_number * shard_len
        scores = score_tile(flat_rows, pieces[turn_number]) * score_scale
        causal = (first_key + jnp.arange(shard_len, dtype=jnp.int32))[None, :] <= flat_places[
            :, None
        ]
        tile_top = jnp.max(jnp.where(causal, scores, masked_score), axis=1)
        new_top = jnp.maximum(running_top, tile_top)
        weights = jnp.where(causal, jnp.exp(scores - new_top[:, None]), 0.0)
        tile_mass = jnp.sum(weights.reshape(row_count, local_blocks, BLOCK), axis=2)
        rescaled = running_mass * jnp.exp(running_top - new_top)[:, None]
        placed = lax.dynamic_update_slice(rescaled, tile_mass, (jnp.int32(0), first_key // BLOCK))
        return (new_top, placed)

    running_top, running_mass = lax.fori_loop(0, pieces.shape[0], absorb_one, initial)
    teacher = running_mass / jnp.sum(running_mass, axis=1, keepdims=True)
    every_key = gather_directly(gate_key, SEQ, 0)
    gate_query = jnp.einsum("hcd,dg->hcg", pooled_query, query_gate_weight, precision=highest)
    local_block = local_places // BLOCK
    gate_rows = jnp.take_along_axis(gate_query, local_block[:, :, None], axis=1).reshape(
        row_count, gate_width
    )
    pooled_rows = jnp.take_along_axis(pooled_query, local_block[:, :, None], axis=1).reshape(
        row_count, head_width
    )
    own_block = flat_places // BLOCK
    allowed = jnp.arange(total_blocks, dtype=jnp.int32)[None, :] <= own_block[:, None]
    logits = jnp.dot(gate_rows, every_key.T, precision=highest) * gate_scale
    logit_top = jnp.max(jnp.where(allowed, logits, masked_score), axis=1)
    gate_weights = jnp.where(allowed, jnp.exp(logits - logit_top[:, None]), 0.0)
    gate_total = jnp.sum(gate_weights, axis=1)
    log_total = logit_top + jnp.log(gate_total)
    flat_loss = log_total - jnp.sum(jnp.where(allowed, teacher * logits, 0.0), axis=1)
    gate_delta = jnp.where(allowed, gate_weights / gate_total[:, None] - teacher, 0.0)
    query_part = jnp.dot(
        pooled_rows.T,
        jnp.dot(gate_delta, every_key, precision=highest) * gate_scale,
        precision=highest,
    )
    key_delta = sent_and_summed(
        jnp.dot(gate_delta.T, gate_rows, precision=highest) * gate_scale, SEQ, 0
    )
    key_part = jnp.dot(pooled_key.T, key_delta, precision=highest)
    row_loss = flat_loss.reshape(head_count, rows_local)
    query_grad, key_grad = in_one((query_part, key_part), SEQ_KV)
    return (row_loss, query_grad, key_grad)


def solution(mesh):
    torus = Mesh(
        mesh.devices.reshape(2, 16, 2, mesh.shape["kv"]), ("seq_0", "seq_1", "seq_2", "kv")
    )
    placed = (P("kv", SEQ, None), P("kv", SEQ, None), P("kv", SEQ), P(), P())
    return jax.shard_map(
        body, mesh=torus, in_specs=placed, out_specs=(P("kv", SEQ), P(), P()), check_vma=False
    )
```

profile of v0, /device:TPU:2, one launch (start us, length us, event | category | flops | bytes accessed | tf_op | source)
XLA Modules:
  0.0 741.4 jit_solution(1190638927435643087)
XLA Ops:
  7.2 6.4 all_gather.9
  13.7 76.9 %all-gather.3.cloned.1.call-done = bf16[32,256,128]{2,1,0:T(8,128)(2,1)} async-done(((bf16[2,256,128]{2,1,0:T(8,128)(2,1)}), bf16[32,256,128]{2,1,0:T(8,128)(2,1)}) %all-gather.3.cloned.1.call-update) | async-done | bytes 2097168 | tf_op jit(solution)/shard_map/all_gather | solution.py:24
  93.3 9.6 %all-to-all-start = ((f32[64,2,128]{2,1,0:T(2,128)}), f32[64,2,128]{2,1,0:T(2,128)S(1)}, u32[]{:S(2)}, u32[]{:S(2)}) async-start(f32[64,2,128]{2,1,0:T(2,128)} %broadcast_in_dim.73), calls=%async_computation | async-start | bytes 131072 | tf_op jit(solution)/shard_map/all_to_all | solution.py:37
  103.6 1.1 convert_reduce_fusion
  110.5 1.7 gather_fusion
  112.3 5.1 all-to-all-done
  117.8 4.7 copy.13
  122.4 125.2 %while.19 = (s32[]{:T(128)}, f32[64]{0:T(128)S(1)}, f32[64,128]{1,0:T(8,128)S(1)}, s32[8,8]{1,0:T(8,128)}, bf16[64,256,128]{2,1,0:T(8,128)(2,1)}, /*index=5*/bf1...) while((s32[]{:T(128)}, f32[64]{0:T(128)S(1)}, ...), condition=%wide.wide.region_9.11_spmd.clone, body=%wide.wide.region_6.10_spmd.clone.sunk | while | flops 4333846 | bytes 548455 | solution.py:121
  130.1 1.1 fusion.39
  136.0 1.1 fusion.39
  145.8 1.1 fusion.39
  151.7 1.1 fusion.39
  157.5 1.1 fusion.39
  167.3 1.1 fusion.39
  173.2 1.1 fusion.39
  183.0 1.1 fusion.39
  188.9 1.1 fusion.39
  194.8 1.1 fusion.39
  204.6 1.1 fusion.39
  248.9 10.0 %all-to-all-start.1 = ((f32[64,2,128]{2,1,0:T(2,128)}), f32[64,2,128]{2,1,0:T(2,128)S(1)}, u32[]{:S(2)}, u32[]{:S(2)}) async-start(f32[64,2,128]{2,1,0:T(2,128)} %bitcast.16), calls=%async_computation.1 | async-start | bytes 131072 | tf_op jit(solution)/shard_map/all_to_all | solution.py:52
  259.7 13.8 %all-to-all-done.1 = f32[64,2,128]{2,1,0:T(2,128)S(1)} async-done(((f32[64,2,128]{2,1,0:T(2,128)}), f32[64,2,128]{2,1,0:T(2,128)S(1)}, u32[]{:S(2)}, u32[]{:S(2)}) %all-to-all-start.1) | async-done | bytes 65568 | tf_op jit(solution)/shard_map/all_to_all | solution.py:52
  275.5 456.2 %all-reduce.2.cloned.1.call-done = f32[65536]{0:T(1024)} async-done(((f32[65536]{0:T(1024)}), f32[65536]{0:T(1024)}) %all-reduce.2.cloned.1.call-update) | async-done | bytes 262160 | tf_op jit(solution)/shard_map/psum | solution.py:60
  731.7 1.6 slice_bitcast_fusion
  733.4 1.5 slice_bitcast_fusion.1
  (545 shorter events, 120.9 us)
Async XLA Ops:
  7.2 85.2 %copy-start = (f32[384,128]{1,0:T(8,128)S(1)}, f32[384,128]{1,0:T(8,128)}, u32[]{:S(2)}) copy-start(f32[384,128]{1,0:T(8,128)} %param.13) | copy-start | bytes 589828
  7.2 83.4 %all-gather.3.cloned.1.call-start = ((), (), s32[]{:S(2)}) async-start(), calls=%async_computation.2 | async-start | bytes 2228224 | tf_op jit(solution)/shard_map/all_gather | solution.py:24
  13.6 104.1 %all-gather.5.cloned.1.call-start = ((), (), s32[]{:S(2)}) async-start(), calls=%async_computation.3 | async-start | bytes 6291456 | tf_op jit(solution)/shard_map/all_gather | solution.py:24
  93.3 24.1 %all-to-all-start = ((f32[64,2,128]{2,1,0:T(2,128)}), f32[64,2,128]{2,1,0:T(2,128)S(1)}, u32[]{:S(2)}, u32[]{:S(2)}) async-start(f32[64,2,128]{2,1,0:T(2,128)} %broadcast_in_dim.73), calls=%async_computation | async-start | bytes 131072 | tf_op jit(solution)/shard_map/all_to_all | solution.py:37
  248.9 24.6 %all-to-all-start.1 = ((f32[64,2,128]{2,1,0:T(2,128)}), f32[64,2,128]{2,1,0:T(2,128)S(1)}, u32[]{:S(2)}, u32[]{:S(2)}) async-start(f32[64,2,128]{2,1,0:T(2,128)} %bitcast.16), calls=%async_computation.1 | async-start | bytes 131072 | tf_op jit(solution)/shard_map/all_to_all | solution.py:52
  259.0 472.7 %all-reduce.2.cloned.1.call-start = ((), (), s32[]{:S(2)}) async-start(), calls=%async_computation.4 | async-start | bytes 524288 | tf_op jit(solution)/shard_map/psum | solution.py:60
Sparse Core Ops, SparseCore 0:
  13.7 76.7 all-gather.2
  92.6 21.0 all-gather.4
  274.9 456.7 all-reduce.1
where the time goes:
time: 745 us; the launch traced here: 741 us
  waiting for transfers between devices  552 us (74%)
  matrix products  74.3 us (10%)
  local copies, waits for them, and re-layouts  42.7 us (6%)
  other arithmetic  26.4 us (4%)
  starting transfers between devices  19.8 us (3%)
  between operations  13.9 us (2%)
    psum x1, waiting for transfers between devices, in_one(): so_far = lax.psum(jnp.concatenate([a.ravel() for a in arrays]), axis)  456 us
    all_gather x2, waiting for transfers between devices, gather_in_order(): tiles = lax.all_gather(tiles, axes[k], axis=0, tiled=True)  76.9 us
    dot_general x64, matrix products, score_tile(): lax.dot_general(row_block, key_block, (((1,), (1,)), ((), ())), preferred...  70.5 us
    dynamic_update_slice x64, local copies, waits for them, and re-layouts, absorb_one(): lax.dynamic_update_slice(rescaled, tile_mass, (jnp.int32(0), first_key //...  26.3 us
  transfers between devices with their start and end apart: 5, of which 4 were waited for; matrix products, arithmetic and copies ran while one was open for 2% of the time, Pallas kernels for 0%

commit v1 on v0

--- a/solution.py
+++ b/solution.py
@@ -21,7 +21,9 @@
 def gather_in_order(array, axes, sequence):
     tiles = array[None]
     for k in sequence:
-        tiles = lax.all_gather(tiles, axes[k], axis=0, tiled=True)
+        tiles = jnp.concatenate(
+            lax.all_to_all(jnp.stack([tiles] * lax.axis_size(axes[k])), axes[k], 0, 0), axis=0
+        )
     held = [lax.axis_size(axes[k]) for k in reversed(sequence)]
     tiles = tiles.reshape(*held, *array.shape)
     turned = sorted(range(len(sequence)), key=lambda place: sequence[len(sequence) - 1 - place])

time: 745 us -> 780 us (1.047)
  blocking collectives: 6.37 us -> 37.5 us
  waiting for transfers between devices: 552 us -> 562 us
    all_to_all x1 -> x2, waiting for transfers between devices: 5.06 us -> 91.6 us  [gather_in_order(): lax.all_to_all(jnp.stack([tiles] * lax.axis_size(axes[k])), axes[k], 0, 0)]
    all_gather x2 -> x0, waiting for transfers between devices: 76.9 us -> none  [gather_in_order(): tiles = lax.all_gather(tiles, axes[k], axis=0, tiled=True)]
    all_to_all x0 -> x2, blocking collectives: none -> 37.5 us  [the longest x1 30.4 us: from_everyone(): return lax.all_to_all(copies, axis, split_axis=0, concat_axis=0, tiled=True)]
  transfers between devices with their start and end apart: 5 -> 4, of which waited for: 4 -> 4; matrix products, arithmetic and copies ran while one was open for 2% -> 1% of each run, Pallas kernels for 0% -> 0%
where the time goes in v1:
time: 780 us; the launch traced here: 776 us
  waiting for transfers between devices  562 us (72%)
  matrix products  73.4 us (9%)
  local copies, waits for them, and re-layouts  39.2 us (5%)
  blocking collectives  37.5 us (5%)
  other arithmetic  25.2 us (3%)
  starting transfers between devices  18.5 us (2%)
  between operations  14.2 us (2%)
    psum x1, waiting for transfers between devices, in_one(): so_far = lax.psum(jnp.concatenate([a.ravel() for a in arrays]), axis)  457 us
    all_to_all x2, waiting for transfers between devices, gather_in_order(): lax.all_to_all(jnp.stack([tiles] * lax.axis_size(axes[k])), axes[k], 0, 0)  91.6 us
    dot_general x64, matrix products, score_tile(): lax.dot_general(row_block, key_block, (((1,), (1,)), ((), ())), preferred...  70.6 us
    all_to_all x1, blocking collectives, from_everyone(): return lax.all_to_all(copies, axis, split_axis=0, concat_axis=0, tiled=True)  30.4 us
    dynamic_update_slice x64, local copies, waits for them, and re-layouts, absorb_one(): lax.dynamic_update_slice(rescaled, tile_mass, (jnp.int32(0), first_key //...  26.3 us
  transfers between devices with their start and end apart: 4, of which 4 were waited for; matrix products, arithmetic and copies ran while one was open for 1% of the time, Pallas kernels for 0%

profile of v1, /device:TPU:2, one launch (start us, length us, event | category | flops | bytes accessed | tf_op | source)
XLA Modules:
  0.0 776.2 jit_solution(2521202650976112621)
XLA Ops:
  7.2 1.6 pad_maximum_fusion.2
  8.8 3.4 all-to-all-start.1
  14.2 2.5 all-to-all-done.1
  16.7 30.4 %all_to_all.25 = f32[64,2,128]{2,1,0:T(2,128)S(1)} all-to-all(f32[64,2,128]{2,1,0:T(2,128)S(1)} %broadcast_in_dim.73), channel_id=1, replica_groups=mesh['seq_0'=2,'seq_1'=16,'seq_2'=2,'kv'=8] {'seq_0','seq_1','seq_2'}, dimensions={0} | all-to-all | bytes 131072 | tf_op jit(solution)/shard_map/all_to_all | solution.py:39
  47.1 1.8 stack.10
  48.9 3.7 all-to-all-start.2
  56.3 89.1 %all-to-all-done.2 = bf16[16,2,256,128]{3,2,1,0:T(8,128)(2,1)S(1)} async-done(((bf16[16,2,256,128]{3,2,1,0:T(8,128)(2,1)}), bf16[16,2,256,128]{3,2,1,0:T(8,128)(2,1)S(1)}, u32[]{:S(2)}, u32[]{:S(2)}) %all-to-all-start.2) | async-done | bytes 2097184 | tf_op jit(solution)/shard_map/all_to_all | solution.py:25
  145.8 7.1 all_to_all.26
  152.9 2.2 copy.14
  155.1 125.1 %while.19 = (s32[]{:T(128)}, f32[64]{0:T(128)S(1)}, f32[64,128]{1,0:T(8,128)S(1)}, s32[8,8]{1,0:T(8,128)}, bf16[64,256,128]{2,1,0:T(8,128)(2,1)}, /*index=5*/bf1...) while((s32[]{:T(128)}, f32[64]{0:T(128)S(1)}, ...), condition=%wide.wide.region_9.11_spmd.clone, body=%wide.wide.region_6.10_spmd.clone.sunk | while | flops 4333846 | bytes 548455 | solution.py:123
  156.9 1.1 fusion.39
  158.9 1.1 fusion.39
  160.8 1.1 fusion.39
  162.8 1.1 fusion.39
  164.7 1.1 fusion.39
  166.7 1.1 fusion.39
  168.7 1.1 fusion.39
  170.6 1.1 fusion.39
  172.6 1.1 fusion.39
  281.6 11.4 %all-to-all-start.4 = ((f32[64,2,128]{2,1,0:T(2,128)}), f32[64,2,128]{2,1,0:T(2,128)S(1)}, u32[]{:S(2)}, u32[]{:S(2)}) async-start(f32[64,2,128]{2,1,0:T(2,128)} %bitcast.19), calls=%async_computation.4 | async-start | bytes 131072 | tf_op jit(solution)/shard_map/all_to_all | solution.py:54
  293.7 13.8 %all-to-all-done.4 = f32[64,2,128]{2,1,0:T(2,128)S(1)} async-done(((f32[64,2,128]{2,1,0:T(2,128)}), f32[64,2,128]{2,1,0:T(2,128)S(1)}, u32[]{:S(2)}, u32[]{:S(2)}) %all-to-all-start.4) | async-done | bytes 65568 | tf_op jit(solution)/shard_map/all_to_all | solution.py:54
  309.5 456.7 %all-reduce.2.cloned.1.call-done = f32[65536]{0:T(1024)} async-done(((f32[65536]{0:T(1024)}), f32[65536]{0:T(1024)}) %all-reduce.2.cloned.1.call-update) | async-done | bytes 262160 | tf_op jit(solution)/shard_map/psum | solution.py:62
  766.2 1.6 slice_bitcast_fusion
  767.9 1.5 slice_bitcast_fusion.1
  (551 shorter events, 119.2 us)
Async XLA Ops:
  7.2 6.8 copy-start
  7.2 45.5 %copy-start.2 = (s32[8,8]{1,0:T(8,128)S(1)}, s32[8,8]{1,0:T(8,128)}, u32[]{:S(2)}) copy-start(s32[8,8]{1,0:T(8,128)} %param.11) | copy-start | bytes 772
  7.2 45.7 %copy-start.1 = (bf16[8,256,128]{2,1,0:T(8,128)(2,1)S(1)}, bf16[8,256,128]{2,1,0:T(8,128)(2,1)}, u32[]{:S(2)}) copy-start(bf16[8,256,128]{2,1,0:T(8,128)(2,1)} %param.9) | copy-start | bytes 1572868
  7.2 45.8 %copy-start.3 = (f32[128,128]{1,0:T(8,128)S(1)}, f32[128,128]{1,0:T(8,128)}, u32[]{:S(2)}) copy-start(f32[128,128]{1,0:T(8,128)} %param.12) | copy-start | bytes 196612
  8.8 7.8 %all-to-all-start.1 = ((bf16[2,1,256,128]{3,2,1,0:T(8,128)(2,1)}), bf16[2,1,256,128]{3,2,1,0:T(8,128)(2,1)S(1)}, u32[]{:S(2)}, u32[]{:S(2)}) async-start(bf16[2,1,256,128]{3,2,1,0:T(8,128)(2,1)} %pad_maximum_fusion.2), calls=%async_computation.1 | async-start | bytes 262144 | tf_op jit(solution)/shard_map/all_to_all | solution.py:25
  48.9 96.5 %all-to-all-start.2 = ((bf16[16,2,256,128]{3,2,1,0:T(8,128)(2,1)}), bf16[16,2,256,128]{3,2,1,0:T(8,128)(2,1)S(1)}, u32[]{:S(2)}, u32[]{:S(2)}) async-start(bf16[16,2,256,128]{3,2,1,0:T(8,128)(2,1)} %stack.10), calls=%async_computation.2 | async-start | bytes 4194304 | tf_op jit(solution)/shard_map/all_to_all | solution.py:25
  281.6 25.9 %all-to-all-start.4 = ((f32[64,2,128]{2,1,0:T(2,128)}), f32[64,2,128]{2,1,0:T(2,128)S(1)}, u32[]{:S(2)}, u32[]{:S(2)}) async-start(f32[64,2,128]{2,1,0:T(2,128)} %bitcast.19), calls=%async_computation.4 | async-start | bytes 131072 | tf_op jit(solution)/shard_map/all_to_all | solution.py:54
  293.0 473.2 %all-reduce.2.cloned.1.call-start = ((), (), s32[]{:S(2)}) async-start(), calls=%async_computation.5 | async-start | bytes 524288 | tf_op jit(solution)/shard_map/psum | solution.py:62
Sparse Core Ops, SparseCore 0:
  309.0 457.2 all-reduce.1
